TPU v7x, 512 devices: a whole 4x4x16 slice. The times are simulated.
512 devices in a mesh: row: 32 (over y_lo, z), col: 16 (over y_hi, x, core).
Axes of the slice: x: 4, y: 4 (y_hi: 2, y_lo: 2; y = y_hi * 2 + y_lo), z: 16, core: 2. Of those that a mesh axis runs over, the one named last changes fastest.
Arguments:
- image: bfloat16 [32, 2048, 2048], P(None, 'row', 'col'), may hold values from -6 to 6
- weight: bfloat16 [3, 3, 32, 32], replicated, may hold values from -0.375 to 0.375
- bias: float32 [32], replicated, may hold values from -3 to 3
- cotangent: bfloat16 [32, 2048, 2048], P(None, 'row', 'col'), may hold values from -60 to 60
Outputs:
- activation: bfloat16 [32, 2048, 2048], P(None, 'row', 'col')
- grad_image: bfloat16 [32, 2048, 2048], P(None, 'row', 'col')
- grad_weight: float32 [3, 3, 32, 32], replicated
- grad_bias: float32 [32], replicated
All inputs are finite; a program needn't handle non-finite values.
Results may differ from a plain program's by a relative error of at most 0.0065.
Values may be sent and summed in bfloat16 or wider, within the bound.
A program may use at most 64 MiB of HBM per device.

v0:
```python
import math
import jax
import jax.numpy as jnp
from jax import lax
from jax.sharding import PartitionSpec as P

DILATION_PIXELS = 16


def from_behind(value, axis, steps):
    count = lax.axis_size(axis)
    initial, last = (max(0, -steps), min(count, count - steps))
    return lax.ppermute(value, axis, [(source, source + steps) for source in range(initial, last)])


def gelu_pair(preact):
    coef = 0.7978845608
    cube = preact * preact * preact
    tval = jnp.tanh(coef * (preact + 0.044715 * cube))
    value = 0.5 * preact * (1.0 + tval)
    slope_val = 0.5 * (1.0 + tval) + 0.5 * preact * (1.0 - tval * tval) * coef * (
        1.0 + 3.0 * 0.044715 * preact * preact
    )
    return (value, slope_val)


def extended(local_block):
    row_count = local_block.shape[1]
    column_count = local_block.shape[2]
    upper_neighbour = from_behind(local_block[:, row_count - DILATION_PIXELS :, :], "row", 1)
    lower_neighbour = from_behind(local_block[:, :DILATION_PIXELS, :], "row", -1)
    tall_block = jnp.concatenate([upper_neighbour, local_block, lower_neighbour], axis=1)
    left_margin = from_behind(tall_block[:, :, column_count - DILATION_PIXELS :], "col", 1)
    right_margin = from_behind(tall_block[:, :, :DILATION_PIXELS], "col", -1)
    return jnp.concatenate([left_margin, tall_block, right_margin], axis=2)


def tap_view(ext, row_offset, column_offset, row_count, column_count):
    start_row = DILATION_PIXELS + row_offset * DILATION_PIXELS
    start_column = DILATION_PIXELS + column_offset * DILATION_PIXELS
    return ext[:, start_row : start_row + row_count, start_column : start_column + column_count]


def row_stack(ext, row_offset, sign_flip, row_count, column_count):
    return jnp.concatenate(
        [
            tap_view(
                ext, sign_flip * row_offset, sign_flip * column_offset, row_count, column_count
            )
            for column_offset in (-1, 0, 1)
        ],
        axis=0,
    )


def shards(image, weight, bias, cotangent):
    row_count = image.shape[1]
    column_count = image.shape[2]
    channels = image.shape[0]
    height_all = row_count * lax.axis_size("row")
    width_all = column_count * lax.axis_size("col")
    scale = 1.0 / math.sqrt(height_all * width_all)
    image_ext = extended(image)
    preact = jnp.zeros(image.shape, jnp.float32) + bias[:, None, None]
    for row_offset in (-1, 0, 1):
        weight_row = jnp.transpose(weight[row_offset + 1], (1, 0, 2)).reshape(
            channels, 3 * channels
        )
        stacked = row_stack(image_ext, row_offset, 1, row_count, column_count)
        preact = preact + jnp.einsum(
            "ok,krq->orq", weight_row, stacked, preferred_element_type=jnp.float32
        )
    value, slope_val = gelu_pair(preact)
    activation = value.astype(jnp.bfloat16)
    preact_gradient = (cotangent.astype(jnp.float32) * slope_val).astype(jnp.bfloat16)
    taps = []
    for row_offset in (-1, 0, 1):
        stacked = row_stack(image_ext, row_offset, 1, row_count, column_count)
        joined = (
            jnp.einsum("orq,krq->ok", preact_gradient, stacked, preferred_element_type=jnp.float32)
            * scale
        )
        taps.append(jnp.transpose(joined.reshape(channels, 3, channels), (1, 0, 2)))
    local_weight = jnp.stack(taps)
    local_bias = jnp.sum(preact_gradient.astype(jnp.float32), axis=(1, 2)) * scale
    grad_weight, grad_bias = lax.psum((local_weight, local_bias), ("row", "col"))
    grad_ext = extended(preact_gradient)
    total = jnp.zeros(image.shape, jnp.float32)
    for row_offset in (-1, 0, 1):
        weight_row = weight[row_offset + 1].reshape(3 * channels, channels)
        stacked = row_stack(grad_ext, row_offset, -1, row_count, column_count)
        total = total + jnp.einsum(
            "kc,krq->crq", weight_row, stacked, preferred_element_type=jnp.float32
        )
    grad_image = total.astype(jnp.bfloat16)
    return (activation, grad_image, grad_weight, grad_bias)


def solution(mesh):
    return jax.shard_map(
        shards,
        mesh=mesh,
        in_specs=(P(None, "row", "col"), P(), P(), P(None, "row", "col")),
        out_specs=(P(None, "row", "col"), P(None, "row", "col"), P(), P()),
        check_vma=False,
    )
```

profile of v0, /device:TPU:1, one launch (start us, length us, event | category | flops | bytes accessed | tf_op | source)
XLA Modules:
  0.0 181.4 jit_solution(1297893469584585609)
XLA Ops:
  0.6 1.4 copy.42
  2.1 4.4 %collective-permute-start = (bf16[32,16,128]{2,0,1:T(8,128)(2,1)S(1)}, bf16[32,16,128]{2,0,1:T(8,128)(2,1)S(1)}, u32[]{:S(2)}, u32[]{:S(2)}) collective-permute-start(bf16[32,16,128]{2,0,1:T(8,128)(2,1)S(1)} %get-tuple-element.42), channel_id=1, source_target_pairs={{0,16},{16,32},{32,48},{48,64},{64,80},{80,96},{96,112},{112,128},... | collective-permute-start | bytes 393224 | tf_op jit(solution)/shard_map/ppermute | solution.py:13
  6.5 1.3 collective-permute-start.1
  7.8 0.6 collective-permute-done
  8.4 0.4 constant_dynamic-update-slice_fusion.1
  8.8 3.6 %collective-permute-done.1 = bf16[32,16,128]{2,0,1:T(8,128)(2,1)S(1)} collective-permute-done((bf16[32,16,128]{2,0,1:T(8,128)(2,1)S(1)}, bf16[32,16,128]{2,0,1:T(8,128)(2,1)S(1)}, u32[]{:S(2)}, u32[]{:S(2)}) %collective-permute-start.1) | collective-permute-done | bytes 131104 | tf_op jit(solution)/shard_map/ppermute | solution.py:13
  12.4 0.3 fusion.68
  12.7 0.8 copy.45
  13.5 0.8 copy.48
  14.4 6.6 %collective-permute-start.3 = (bf16[32,96,16]{1,2,0:T(8,128)(2,1)S(1)}, bf16[32,96,16]{1,2,0:T(8,128)(2,1)S(1)}, u32[]{:S(2)}, u32[]{:S(2)}) collective-permute-start(bf16[32,96,16]{1,2,0:T(8,128)(2,1)S(1)} %copy.48), channel_id=1, source_target_pairs={{1,0},{2,1},{3,2},{4,3},{5,4},{6,5},{7,6},{8,7},{9,8},{10,9},{11,1... | collective-permute-start | bytes 294920 | tf_op jit(solution)/shard_map/ppermute | solution.py:13
  21.0 1.9 %collective-permute-start.2 = (bf16[32,96,16]{1,2,0:T(8,128)(2,1)S(1)}, bf16[32,96,16]{1,2,0:T(8,128)(2,1)S(1)}, u32[]{:S(2)}, u32[]{:S(2)}) collective-permute-start(bf16[32,96,16]{1,2,0:T(8,128)(2,1)S(1)} %copy.45), channel_id=1, source_target_pairs={{0,1},{1,2},{2,3},{3,4},{4,5},{5,6},{6,7},{7,8},{8,9},{9,10},{10,1... | collective-permute-start | bytes 294920 | tf_op jit(solution)/shard_map/ppermute | solution.py:13
  22.9 1.4 fusion.71
  24.5 0.7 reshape.34
  25.3 1.1 copy.46
  26.4 1.1 copy.49
  27.5 1.1 fusion.54
  28.7 0.3 fusion.50
  29.1 0.6 fusion.10
  29.7 0.2 copy-done.5
  30.0 0.4 fusion.31
  30.3 0.7 copy-done.11
  31.0 2.1 %convert_reduce_fusion = (f32[32]{0:T(128)S(1)}, bf16[32,64,128]{2,0,1:T(8,128)(2,1)S(1)}, bf16[32,64,128]{2,0,1:T(8,128)(2,1)}) fusion(bf16[32,64,128]{2,1,0:T(8,128)(2,1)S(1)} %copy-done.11, f32[64,128,32]{1,2,0:T(8,128)S(1)} %fusion.31, bf16[32,96,1]{1,0,2:T(8,128)(2,1)S(1)} %reshape.35, bf16[96,64,128]{2,0,1:T(8,128)(2,1)S(1)} %fusion.10), kind=kOutput, calls=%fused_computation.64 | convolution fusion | flops 56885216 | bytes 4200576 | tf_op jit(solution)/shard_map/ok,krq->orq/dot_general | solution.py:70
  33.1 0.6 fusion.38
  33.7 0.6 fusion.39
  34.5 0.3 copy-done.2
  34.8 0.6 fusion.40
  35.6 1.3 collective-permute-start.5
  36.9 4.0 %collective-permute-start.4 = (bf16[32,16,128]{2,0,1:T(8,128)(2,1)S(1)}, bf16[32,16,128]{2,0,1:T(8,128)(2,1)S(1)}, u32[]{:S(2)}, u32[]{:S(2)}) collective-permute-start(bf16[32,16,128]{2,0,1:T(8,128)(2,1)S(1)} %get-tuple-element.40), channel_id=1, source_target_pairs={{0,16},{16,32},{32,48},{48,64},{64,80},{80,96},{96,112},{112,128},... | collective-permute-start | bytes 393224 | tf_op jit(solution)/shard_map/ppermute | solution.py:13
  41.0 1.1 collective-permute-done.5
  42.1 0.8 collective-permute-done.4
  43.0 0.3 fusion.67
  43.3 0.8 copy.56
  44.1 0.8 copy.58
  44.9 5.1 %collective-permute-start.7 = (bf16[32,96,16]{1,2,0:T(8,128)(2,1)S(1)}, bf16[32,96,16]{1,2,0:T(8,128)(2,1)S(1)}, u32[]{:S(2)}, u32[]{:S(2)}) collective-permute-start(bf16[32,96,16]{1,2,0:T(8,128)(2,1)S(1)} %copy.58), channel_id=1, source_target_pairs={{0,1},{1,2},{2,3},{3,4},{4,5},{5,6},{6,7},{7,8},{8,9},{9,10},{10,1... | collective-permute-start | bytes 294920 | tf_op jit(solution)/shard_map/ppermute | solution.py:13
  50.0 2.1 %collective-permute-start.6 = (bf16[32,96,16]{1,2,0:T(8,128)(2,1)S(1)}, bf16[32,96,16]{1,2,0:T(8,128)(2,1)S(1)}, u32[]{:S(2)}, u32[]{:S(2)}) collective-permute-start(bf16[32,96,16]{1,2,0:T(8,128)(2,1)S(1)} %copy.56), channel_id=1, source_target_pairs={{1,0},{2,1},{3,2},{4,3},{5,4},{6,5},{7,6},{8,7},{9,8},{10,9},{11,1... | collective-permute-start | bytes 294920 | tf_op jit(solution)/shard_map/ppermute | solution.py:13
  52.2 120.2 %all-reduce = (f32[3,3,32,32]{3,1,2,0:T(4,128)S(1)}, f32[32]{0:T(128)}) all-reduce(f32[3,3,32,32]{3,1,2,0:T(4,128)S(1)} %pad_maximum_fusion.11, f32[32]{0:T(128)S(1)} %broadcast_multiply_fusion), channel_id=1, replica_groups=mesh['row'=32,'col'=16] {'row','col'}, use_global_device_ids=true, to_apply=%region_0.0 | all-reduce | flops 9248 | bytes 73984 | tf_op jit(solution)/shard_map/psum | solution.py:86
  172.4 0.7 copy.65
  173.1 1.0 copy.63
  174.1 1.1 copy.57
  175.2 1.1 copy.59
  176.3 1.5 pad_maximum_fusion.7
  177.8 0.7 fusion.65
  178.5 0.4 fusion.16
  178.9 0.4 copy-done.8
  179.3 0.4 fusion.2
  179.7 0.4 copy-done.7
  180.0 0.4 fusion.35
  180.4 1.0 copy.64
  (40 shorter events, 0.9 us)
Async XLA Ops:
  0.6 7.8 %copy-start = (bf16[32,64,128]{2,1,0:T(8,128)(2,1)S(1)}, bf16[32,64,128]{2,1,0:T(8,128)(2,1)}, u32[]{:S(2)}) copy-start(bf16[32,64,128]{2,1,0:T(8,128)(2,1)} %param.4) | copy-start | bytes 1572868
  2.1 6.3 %collective-permute-start = (bf16[32,16,128]{2,0,1:T(8,128)(2,1)S(1)}, bf16[32,16,128]{2,0,1:T(8,128)(2,1)S(1)}, u32[]{:S(2)}, u32[]{:S(2)}) collective-permute-start(bf16[32,16,128]{2,0,1:T(8,128)(2,1)S(1)} %get-tuple-element.42), channel_id=1, source_target_pairs={{0,16},{16,32},{32,48},{48,64},{64,80},{80,96},{96,112},{112,128},... | collective-permute-start | bytes 393224 | tf_op jit(solution)/shard_map/ppermute | solution.py:13
  6.5 5.9 %collective-permute-start.1 = (bf16[32,16,128]{2,0,1:T(8,128)(2,1)S(1)}, bf16[32,16,128]{2,0,1:T(8,128)(2,1)S(1)}, u32[]{:S(2)}, u32[]{:S(2)}) collective-permute-start(bf16[32,16,128]{2,0,1:T(8,128)(2,1)S(1)} %get-tuple-element.41), channel_id=1, source_target_pairs={{16,0},{32,16},{48,32},{64,48},{80,64},{96,80},{112,96},{128,112},... | collective-permute-start | bytes 393224 | tf_op jit(solution)/shard_map/ppermute | solution.py:13
  8.4 4.3 %copy-start.4 = (bf16[32,16,128]{2,0,1:T(8,128)(2,1)}, bf16[32,16,128]{2,0,1:T(8,128)(2,1)S(1)}, u32[]{:S(2)}) copy-start(bf16[32,16,128]{2,0,1:T(8,128)(2,1)S(1)} %collective-permute-done) | copy-start | bytes 393220
  14.4 12.0 %collective-permute-start.3 = (bf16[32,96,16]{1,2,0:T(8,128)(2,1)S(1)}, bf16[32,96,16]{1,2,0:T(8,128)(2,1)S(1)}, u32[]{:S(2)}, u32[]{:S(2)}) collective-permute-start(bf16[32,96,16]{1,2,0:T(8,128)(2,1)S(1)} %copy.48), channel_id=1, source_target_pairs={{1,0},{2,1},{3,2},{4,3},{5,4},{6,5},{7,6},{8,7},{9,8},{10,9},{11,1... | collective-permute-start | bytes 294920 | tf_op jit(solution)/shard_map/ppermute | solution.py:13
  21.0 4.3 %collective-permute-start.2 = (bf16[32,96,16]{1,2,0:T(8,128)(2,1)S(1)}, bf16[32,96,16]{1,2,0:T(8,128)(2,1)S(1)}, u32[]{:S(2)}, u32[]{:S(2)}) collective-permute-start(bf16[32,96,16]{1,2,0:T(8,128)(2,1)S(1)} %copy.45), channel_id=1, source_target_pairs={{0,1},{1,2},{2,3},{3,4},{4,5},{5,6},{6,7},{7,8},{8,9},{9,10},{10,1... | collective-permute-start | bytes 294920 | tf_op jit(solution)/shard_map/ppermute | solution.py:13
  27.5 1.2 copy-start.10
  28.7 1.0 copy-start.1
  29.1 0.9 copy-start.5
  29.1 0.9 copy-start.12
  30.0 1.0 copy-start.11
  33.7 1.1 copy-start.2
  33.7 1.1 copy-start.6
  35.6 6.5 %collective-permute-start.5 = (bf16[32,16,128]{2,0,1:T(8,128)(2,1)S(1)}, bf16[32,16,128]{2,0,1:T(8,128)(2,1)S(1)}, u32[]{:S(2)}, u32[]{:S(2)}) collective-permute-start(bf16[32,16,128]{2,0,1:T(8,128)(2,1)S(1)} %get-tuple-element.39), channel_id=1, source_target_pairs={{16,0},{32,16},{48,32},{64,48},{80,64},{96,80},{112,96},{128,112},... | collective-permute-start | bytes 393224 | tf_op jit(solution)/shard_map/ppermute | solution.py:13
  36.9 5.9 %collective-permute-start.4 = (bf16[32,16,128]{2,0,1:T(8,128)(2,1)S(1)}, bf16[32,16,128]{2,0,1:T(8,128)(2,1)S(1)}, u32[]{:S(2)}, u32[]{:S(2)}) collective-permute-start(bf16[32,16,128]{2,0,1:T(8,128)(2,1)S(1)} %get-tuple-element.40), channel_id=1, source_target_pairs={{0,16},{16,32},{32,48},{48,64},{64,80},{80,96},{96,112},{112,128},... | collective-permute-start | bytes 393224 | tf_op jit(solution)/shard_map/ppermute | solution.py:13
  43.3 129.8 %copy-start.3 = (bf16[32,64,128]{2,0,1:T(8,128)(2,1)S(1)}, bf16[32,64,128]{2,0,1:T(8,128)(2,1)}, u32[]{:S(2)}) copy-start(bf16[32,64,128]{2,0,1:T(8,128)(2,1)} %get-tuple-element.30) | copy-start | bytes 1572868
  44.9 130.3 %collective-permute-start.7 = (bf16[32,96,16]{1,2,0:T(8,128)(2,1)S(1)}, bf16[32,96,16]{1,2,0:T(8,128)(2,1)S(1)}, u32[]{:S(2)}, u32[]{:S(2)}) collective-permute-start(bf16[32,96,16]{1,2,0:T(8,128)(2,1)S(1)} %copy.58), channel_id=1, source_target_pairs={{0,1},{1,2},{2,3},{3,4},{4,5},{5,6},{6,7},{7,8},{8,9},{9,10},{10,1... | collective-permute-start | bytes 294920 | tf_op jit(solution)/shard_map/ppermute | solution.py:13
  50.0 124.1 %collective-permute-start.6 = (bf16[32,96,16]{1,2,0:T(8,128)(2,1)S(1)}, bf16[32,96,16]{1,2,0:T(8,128)(2,1)S(1)}, u32[]{:S(2)}, u32[]{:S(2)}) collective-permute-start(bf16[32,96,16]{1,2,0:T(8,128)(2,1)S(1)} %copy.56), channel_id=1, source_target_pairs={{1,0},{2,1},{3,2},{4,3},{5,4},{6,5},{7,6},{8,7},{9,8},{10,9},{11,1... | collective-permute-start | bytes 294920 | tf_op jit(solution)/shard_map/ppermute | solution.py:13
  177.8 0.7 copy-start.9
  178.5 0.7 copy-start.8
  179.3 0.7 copy-start.7
where the time goes:
time: 182 us; the launch traced here: 181 us
  blocking collectives  120 us (66%)
  starting transfers between devices  26.7 us (15%)
  local copies, waits for them, and re-layouts  18.2 us (10%)
  waiting for transfers between devices  6.11 us (3%)
  matrix products  5.82 us (3%)
  other arithmetic  3.41 us (2%)
    psum x1, blocking collectives, shards(): lax.psum((local_weight, local_bias), ('row', 'col'))  120 us
    ppermute x8, starting transfers between devices, from_behind(): lax.ppermute(value, axis, [(source, source + steps) for source in range(i...  26.7 us
    unnamed x32, local copies, waits for them, and re-layouts  6.49 us
    ppermute x8, waiting for transfers between devices, from_behind(): lax.ppermute(value, axis, [(source, source + steps) for source in range(i...  6.11 us
    ppermute x4, local copies, waits for them, and re-layouts, from_behind(): lax.ppermute(value, axis, [(source, source + steps) for source in range(i...  4.41 us
  transfers between devices with their start and end apart: 8, of which 4 were waited for; matrix products, arithmetic and copies ran while one was open for 4% of the time, Pallas kernels for 0%

commit v1 on v0

--- a/solution.py
+++ b/solution.py
@@ -83,7 +83,13 @@
         taps.append(jnp.transpose(joined.reshape(channels, 3, channels), (1, 0, 2)))
     local_weight = jnp.stack(taps)
     local_bias = jnp.sum(preact_gradient.astype(jnp.float32), axis=(1, 2)) * scale
-    grad_weight, grad_bias = lax.psum((local_weight, local_bias), ("row", "col"))
+
+    def rounds_produce(my_data, peer_axis, bus_axis="row"):
+        for tick in (peer_axis, bus_axis):
+            my_data = lax.psum(my_data, tick)
+        return my_data
+
+    grad_weight, grad_bias = rounds_produce((local_weight, local_bias), "col")
     grad_ext = extended(preact_gradient)
     total = jnp.zeros(image.shape, jnp.float32)
     for row_offset in (-1, 0, 1):

time: 182 us -> 267 us (1.47)
  the two profiles are of different devices: /device:TPU:1 before, /device:TPU:24 now
where the time goes in v1:
time: 267 us
  blocking collectives  187 us (70%)
  starting transfers between devices  36.2 us (14%)
  local copies, waits for them, and re-layouts  18.2 us (7%)
  waiting for transfers between devices  15 us (6%)
  matrix products  5.81 us (2%)
  other arithmetic  3.41 us (1%)
    psum x2, blocking collectives, rounds_produce(): my_data = lax.psum(my_data, tick)  187 us
    ppermute x8, starting transfers between devices, from_behind(): lax.ppermute(value, axis, [(source, source + steps) for source in range(i...  36.2 us
    ppermute x8, waiting for transfers between devices, from_behind(): lax.ppermute(value, axis, [(source, source + steps) for source in range(i...  15 us
    unnamed x32, local copies, waits for them, and re-layouts  6.49 us
  transfers between devices with their start and end apart: 8, of which 5 were waited for; matrix products, arithmetic and copies ran while one was open for 2% of the time, Pallas kernels for 0%

profile of v1, /device:TPU:24, one launch (start us, length us, event | category | flops | bytes accessed | tf_op | source)
XLA Modules:
  0.0 266.7 jit_solution(816818120320261366)
XLA Ops:
  0.6 1.4 copy.42
  2.1 3.8 %collective-permute-start = (bf16[32,16,128]{2,0,1:T(8,128)(2,1)S(1)}, bf16[32,16,128]{2,0,1:T(8,128)(2,1)S(1)}, u32[]{:S(2)}, u32[]{:S(2)}) collective-permute-start(bf16[32,16,128]{2,0,1:T(8,128)(2,1)S(1)} %get-tuple-element.44), channel_id=1, source_target_pairs={{0,16},{16,32},{32,48},{48,64},{64,80},{80,96},{96,112},{112,128},... | collective-permute-start | bytes 393224 | tf_op jit(solution)/shard_map/ppermute | solution.py:13
  6.0 9.7 %collective-permute-start.1 = (bf16[32,16,128]{2,0,1:T(8,128)(2,1)S(1)}, bf16[32,16,128]{2,0,1:T(8,128)(2,1)S(1)}, u32[]{:S(2)}, u32[]{:S(2)}) collective-permute-start(bf16[32,16,128]{2,0,1:T(8,128)(2,1)S(1)} %get-tuple-element.43), channel_id=1, source_target_pairs={{16,0},{32,16},{48,32},{64,48},{80,64},{96,80},{112,96},{128,112},... | collective-permute-start | bytes 393224 | tf_op jit(solution)/shard_map/ppermute | solution.py:13
  15.6 1.6 collective-permute-done
  17.2 0.4 constant_dynamic-update-slice_fusion.1
  17.6 0.8 collective-permute-done.1
  18.4 0.3 fusion.68
  18.7 0.8 copy.45
  19.5 0.8 copy.48
  20.4 3.6 %collective-permute-start.3 = (bf16[32,96,16]{1,2,0:T(8,128)(2,1)S(1)}, bf16[32,96,16]{1,2,0:T(8,128)(2,1)S(1)}, u32[]{:S(2)}, u32[]{:S(2)}) collective-permute-start(bf16[32,96,16]{1,2,0:T(8,128)(2,1)S(1)} %copy.48), channel_id=1, source_target_pairs={{1,0},{2,1},{3,2},{4,3},{5,4},{6,5},{7,6},{8,7},{9,8},{10,9},{11,1... | collective-permute-start | bytes 294920 | tf_op jit(solution)/shard_map/ppermute | solution.py:13
  24.0 1.9 collective-permute-start.2
  25.9 1.4 fusion.71
  27.5 0.7 reshape.34
  28.3 5.6 %collective-permute-done.2 = bf16[32,96,16]{1,2,0:T(8,128)(2,1)S(1)} collective-permute-done((bf16[32,96,16]{1,2,0:T(8,128)(2,1)S(1)}, bf16[32,96,16]{1,2,0:T(8,128)(2,1)S(1)}, u32[]{:S(2)}, u32[]{:S(2)}) %collective-permute-start.2) | collective-permute-done | bytes 98336 | tf_op jit(solution)/shard_map/ppermute | solution.py:13
  33.9 1.1 copy.46
  35.0 1.1 copy.49
  36.1 1.1 fusion.54
  37.3 0.3 fusion.50
  37.7 0.6 fusion.10
  38.6 0.4 fusion.31
  38.9 0.7 copy-done.11
  39.6 2.1 convert_reduce_fusion
  41.7 0.6 fusion.38
  42.3 0.6 fusion.39
  43.4 0.6 fusion.40
  44.2 5.9 %collective-permute-start.5 = (bf16[32,16,128]{2,0,1:T(8,128)(2,1)S(1)}, bf16[32,16,128]{2,0,1:T(8,128)(2,1)S(1)}, u32[]{:S(2)}, u32[]{:S(2)}) collective-permute-start(bf16[32,16,128]{2,0,1:T(8,128)(2,1)S(1)} %get-tuple-element.41), channel_id=1, source_target_pairs={{16,0},{32,16},{48,32},{64,48},{80,64},{96,80},{112,96},{128,112},... | collective-permute-start | bytes 393224 | tf_op jit(solution)/shard_map/ppermute | solution.py:13
  50.1 1.9 collective-permute-start.4
  52.1 0.6 collective-permute-done.5
  52.6 6.5 %collective-permute-done.4 = bf16[32,16,128]{2,0,1:T(8,128)(2,1)S(1)} collective-permute-done((bf16[32,16,128]{2,0,1:T(8,128)(2,1)S(1)}, bf16[32,16,128]{2,0,1:T(8,128)(2,1)S(1)}, u32[]{:S(2)}, u32[]{:S(2)}) %collective-permute-start.4) | collective-permute-done | bytes 131104 | tf_op jit(solution)/shard_map/ppermute | solution.py:13
  59.2 0.3 fusion.67
  59.5 0.8 copy.56
  60.3 0.8 copy.58
  61.2 1.9 collective-permute-start.7
  63.1 7.4 %collective-permute-start.6 = (bf16[32,96,16]{1,2,0:T(8,128)(2,1)S(1)}, bf16[32,96,16]{1,2,0:T(8,128)(2,1)S(1)}, u32[]{:S(2)}, u32[]{:S(2)}) collective-permute-start(bf16[32,96,16]{1,2,0:T(8,128)(2,1)S(1)} %copy.56), channel_id=1, source_target_pairs={{1,0},{2,1},{3,2},{4,3},{5,4},{6,5},{7,6},{8,7},{9,8},{10,9},{11,1... | collective-permute-start | bytes 294920 | tf_op jit(solution)/shard_map/ppermute | solution.py:13
  70.6 67.2 %all-reduce.1 = (f32[3,3,32,32]{3,1,2,0:T(4,128)S(1)}, f32[32]{0:T(128)S(1)}) all-reduce(f32[3,3,32,32]{3,1,2,0:T(4,128)S(1)} %pad_maximum_fusion.11, f32[32]{0:T(128)S(1)} %broadcast_multiply_fusion), channel_id=1, replica_groups=mesh['row'=32,'col'=16] {'col'}, use_global_device_ids=true, to_apply=%region_0.0 | all-reduce | flops 9248 | bytes 73984 | tf_op jit(solution)/shard_map/psum | solution.py:89
  137.8 119.8 %all-reduce = (f32[3,3,32,32]{3,1,2,0:T(4,128)S(1)}, f32[32]{0:T(128)}) all-reduce(f32[3,3,32,32]{3,1,2,0:T(4,128)S(1)} %get-tuple-element.18, f32[32]{0:T(128)S(1)} %get-tuple-element.19), channel_id=1, replica_groups=mesh['row'=32,'col'=16] {'row'}, use_global_device_ids=true, to_apply=%region_1.0 | all-reduce | flops 9248 | bytes 73984 | tf_op jit(solution)/shard_map/psum | solution.py:89
  257.7 0.7 copy.65
  258.4 1.0 copy.63
  259.4 1.1 copy.57
  260.5 1.1 copy.59
  261.6 1.5 pad_maximum_fusion.7
  263.1 0.7 fusion.65
  263.8 0.4 fusion.16
  264.2 0.4 copy-done.8
  264.6 0.4 fusion.2
  264.9 0.4 copy-done.7
  265.3 0.4 fusion.35
  265.7 1.0 copy.64
  (41 shorter events, 1.4 us)
Async XLA Ops:
  0.6 16.6 %copy-start = (bf16[32,64,128]{2,1,0:T(8,128)(2,1)S(1)}, bf16[32,64,128]{2,1,0:T(8,128)(2,1)}, u32[]{:S(2)}) copy-start(bf16[32,64,128]{2,1,0:T(8,128)(2,1)} %param.4) | copy-start | bytes 1572868
  2.1 15.1 %collective-permute-start = (bf16[32,16,128]{2,0,1:T(8,128)(2,1)S(1)}, bf16[32,16,128]{2,0,1:T(8,128)(2,1)S(1)}, u32[]{:S(2)}, u32[]{:S(2)}) collective-permute-start(bf16[32,16,128]{2,0,1:T(8,128)(2,1)S(1)} %get-tuple-element.44), channel_id=1, source_target_pairs={{0,16},{16,32},{32,48},{48,64},{64,80},{80,96},{96,112},{112,128},... | collective-permute-start | bytes 393224 | tf_op jit(solution)/shard_map/ppermute | solution.py:13
  6.0 12.4 %collective-permute-start.1 = (bf16[32,16,128]{2,0,1:T(8,128)(2,1)S(1)}, bf16[32,16,128]{2,0,1:T(8,128)(2,1)S(1)}, u32[]{:S(2)}, u32[]{:S(2)}) collective-permute-start(bf16[32,16,128]{2,0,1:T(8,128)(2,1)S(1)} %get-tuple-element.43), channel_id=1, source_target_pairs={{16,0},{32,16},{48,32},{64,48},{80,64},{96,80},{112,96},{128,112},... | collective-permute-start | bytes 393224 | tf_op jit(solution)/shard_map/ppermute | solution.py:13
  17.2 1.5 copy-start.4
  20.4 14.6 %collective-permute-start.3 = (bf16[32,96,16]{1,2,0:T(8,128)(2,1)S(1)}, bf16[32,96,16]{1,2,0:T(8,128)(2,1)S(1)}, u32[]{:S(2)}, u32[]{:S(2)}) collective-permute-start(bf16[32,96,16]{1,2,0:T(8,128)(2,1)S(1)} %copy.48), channel_id=1, source_target_pairs={{1,0},{2,1},{3,2},{4,3},{5,4},{6,5},{7,6},{8,7},{9,8},{10,9},{11,1... | collective-permute-start | bytes 294920 | tf_op jit(solution)/shard_map/ppermute | solution.py:13
  24.0 9.9 %collective-permute-start.2 = (bf16[32,96,16]{1,2,0:T(8,128)(2,1)S(1)}, bf16[32,96,16]{1,2,0:T(8,128)(2,1)S(1)}, u32[]{:S(2)}, u32[]{:S(2)}) collective-permute-start(bf16[32,96,16]{1,2,0:T(8,128)(2,1)S(1)} %copy.45), channel_id=1, source_target_pairs={{0,1},{1,2},{2,3},{3,4},{4,5},{5,6},{6,7},{7,8},{8,9},{9,10},{10,1... | collective-permute-start | bytes 294920 | tf_op jit(solution)/shard_map/ppermute | solution.py:13
  36.1 1.2 copy-start.10
  37.3 1.0 copy-start.1
  37.6 0.9 copy-start.5
  37.7 0.9 copy-start.12
  38.6 1.0 copy-start.11
  42.3 1.1 copy-start.2
  42.3 1.1 copy-start.6
  44.2 8.4 %collective-permute-start.5 = (bf16[32,16,128]{2,0,1:T(8,128)(2,1)S(1)}, bf16[32,16,128]{2,0,1:T(8,128)(2,1)S(1)}, u32[]{:S(2)}, u32[]{:S(2)}) collective-permute-start(bf16[32,16,128]{2,0,1:T(8,128)(2,1)S(1)} %get-tuple-element.41), channel_id=1, source_target_pairs={{16,0},{32,16},{48,32},{64,48},{80,64},{96,80},{112,96},{128,112},... | collective-permute-start | bytes 393224 | tf_op jit(solution)/shard_map/ppermute | solution.py:13
  50.1 9.0 %collective-permute-start.4 = (bf16[32,16,128]{2,0,1:T(8,128)(2,1)S(1)}, bf16[32,16,128]{2,0,1:T(8,128)(2,1)S(1)}, u32[]{:S(2)}, u32[]{:S(2)}) collective-permute-start(bf16[32,16,128]{2,0,1:T(8,128)(2,1)S(1)} %get-tuple-element.42), channel_id=1, source_target_pairs={{0,16},{16,32},{32,48},{48,64},{64,80},{80,96},{96,112},{112,128},... | collective-permute-start | bytes 393224 | tf_op jit(solution)/shard_map/ppermute | solution.py:13
  59.5 198.8 %copy-start.3 = (bf16[32,64,128]{2,0,1:T(8,128)(2,1)S(1)}, bf16[32,64,128]{2,0,1:T(8,128)(2,1)}, u32[]{:S(2)}) copy-start(bf16[32,64,128]{2,0,1:T(8,128)(2,1)} %get-tuple-element.32) | copy-start | bytes 1572868
  61.2 199.3 %collective-permute-start.7 = (bf16[32,96,16]{1,2,0:T(8,128)(2,1)S(1)}, bf16[32,96,16]{1,2,0:T(8,128)(2,1)S(1)}, u32[]{:S(2)}, u32[]{:S(2)}) collective-permute-start(bf16[32,96,16]{1,2,0:T(8,128)(2,1)S(1)} %copy.58), channel_id=1, source_target_pairs={{0,1},{1,2},{2,3},{3,4},{4,5},{5,6},{6,7},{7,8},{8,9},{9,10},{10,1... | collective-permute-start | bytes 294920 | tf_op jit(solution)/shard_map/ppermute | solution.py:13
  63.1 196.3 %collective-permute-start.6 = (bf16[32,96,16]{1,2,0:T(8,128)(2,1)S(1)}, bf16[32,96,16]{1,2,0:T(8,128)(2,1)S(1)}, u32[]{:S(2)}, u32[]{:S(2)}) collective-permute-start(bf16[32,96,16]{1,2,0:T(8,128)(2,1)S(1)} %copy.56), channel_id=1, source_target_pairs={{1,0},{2,1},{3,2},{4,3},{5,4},{6,5},{7,6},{8,7},{9,8},{10,9},{11,1... | collective-permute-start | bytes 294920 | tf_op jit(solution)/shard_map/ppermute | solution.py:13
  263.1 0.7 copy-start.9
  263.8 0.7 copy-start.8
  264.6 0.7 copy-start.7
